TPU v7x, 256 devices: a whole 4x4x8 slice. The times are simulated.
256 devices in a mesh: block: 8 (over z), tile: 32 (over x, y, core).
Axes of the slice: x: 4, y: 4, z: 8, core: 2. Of those that a mesh axis runs over, the one named last changes fastest.
Arguments:
- acts: bfloat16 [16, 32, 64, 384], P('block', 'tile'), may hold values from -6 to 6
- gamma: float32 [384], replicated, may hold values from 0.25 to 1.75
- beta: float32 [384], replicated, may hold values from -3 to 3
- weights: bfloat16 [384, 27, 192], P('tile'), may hold values from -0.0625 to 0.0625
- cotangent: bfloat16 [16, 64, 128, 192], P('block', 'tile'), may hold values from -6 to 6
Outputs:
- d_acts: bfloat16 [16, 32, 64, 384], P('block', 'tile')
- d_weights: float32 [384, 27, 192], P('tile')
All inputs are finite; a program needn't handle non-finite values.
Results may differ from a plain program's by a relative error of at most 0.0029.
Values may be sent and summed in bfloat16 or wider, within the bound.
A program may use at most 128 MiB of HBM per device.

v0:
```python
import jax
import jax.numpy as jnp
from jax import lax
from jax.sharding import PartitionSpec as P

GROUPS = 32
norm_eps = 1e-06


def from_behind(value, axis, steps):
    count = lax.axis_size(axis)
    first, last = (max(0, -steps), min(count, count - steps))
    return lax.ppermute(value, axis, [(source, source + steps) for source in range(first, last)])


def padded_2(value, sides, width):
    for axis, dim in sides:
        size, length = (lax.axis_size(axis), value.shape[dim])
        up = [(i, (i + 1) % size) for i in range(size - 1)]
        down = [(j, i) for i, j in up]
        last = lax.slice_in_dim(value, length - width, length, axis=dim)
        first = lax.slice_in_dim(value, 0, width, axis=dim)
        before = lax.ppermute(last, axis, up)
        after = lax.ppermute(first, axis, down)
        value = jnp.concatenate([before, value, after], axis=dim)
    return value


def group_totals(values, frames, per_group):
    return jnp.sum(values, axis=(1, 2)).reshape(frames, GROUPS, per_group).sum(-1)


def shards(acts, gamma, beta, weights, cotangent):
    frames, low_rows, low_cols, channels = acts.shape
    tiles = lax.axis_size("tile")
    per_group = channels // GROUPS
    group_size = low_rows * tiles * low_cols * per_group
    acts_wide = acts.astype(jnp.float32)
    stat_sum = group_totals(acts_wide, frames, per_group)
    stat_sq = group_totals(acts_wide * acts_wide, frames, per_group)
    stat_sum, stat_sq = lax.psum((stat_sum, stat_sq), "tile")
    group_mean = stat_sum / group_size
    inv_std = lax.rsqrt(stat_sq / group_size - group_mean * group_mean + norm_eps)
    mean_chan = jnp.repeat(group_mean, per_group, axis=1)[:, None, None, :]
    inv_chan = jnp.repeat(inv_std, per_group, axis=1)[:, None, None, :]
    normed = (acts_wide - mean_chan) * inv_chan
    shifted = normed * gamma + beta
    gate_value = jax.nn.sigmoid(shifted)
    hidden = (shifted * gate_value).astype(jnp.bfloat16)
    previous = from_behind(hidden, "block", 1)
    joined = jnp.concatenate([previous, hidden], 0)
    padded = padded_2(joined, (("tile", 1),), 1)
    upsampled = jnp.repeat(jnp.repeat(padded, 2, axis=1), 2, axis=2)[:, 1 : 2 * low_rows + 3]
    upsampled = jnp.pad(upsampled, ((0, 0), (0, 0), (1, 1), (0, 0)))
    following = from_behind(cotangent, "block", -1)
    grad_field = jnp.concatenate([cotangent, following], 0)
    grad_field = padded_2(grad_field, (("tile", 1),), 1)
    grad_field = jnp.pad(grad_field, ((0, 0), (0, 0), (1, 1), (0, 0)))
    up_rows = 2 * low_rows
    up_cols = 2 * low_cols
    num_cells = frames * up_rows * up_cols
    tap_list = [(tap // 9, tap // 3 % 3, tap % 3) for tap in range(27)]
    windows = [
        grad_field[
            2 - tap_t : 2 - tap_t + frames,
            2 - tap_h : 2 - tap_h + up_rows,
            2 - tap_w : 2 - tap_w + up_cols,
        ].reshape(num_cells, -1)
        for tap_t, tap_h, tap_w in tap_list
    ]
    columns = jnp.concatenate(windows, 1)
    piece_rows = lax.all_gather(weights, "tile", axis=0, tiled=True)
    flat_rows = piece_rows.reshape(piece_rows.shape[0], -1)
    back_grad = lax.dot_general(
        columns, flat_rows, (((1,), (1,)), ((), ())), preferred_element_type=jnp.float32
    )
    back_grad = back_grad.reshape(frames, low_rows, 2, low_cols, 2, piece_rows.shape[0])
    act_grad = back_grad.sum(axis=(2, 4))
    silu_slope = gate_value * (1.0 + shifted * (1.0 - gate_value))
    norm_grad = act_grad * silu_slope * gamma
    first_sum = group_totals(norm_grad, frames, per_group)
    second_sum = group_totals(norm_grad * normed, frames, per_group)
    first_sum, second_sum = lax.psum((first_sum, second_sum), "tile")
    first_chan = jnp.repeat(first_sum / group_size, per_group, axis=1)[:, None, None, :]
    second_chan = jnp.repeat(second_sum / group_size, per_group, axis=1)[:, None, None, :]
    d_acts = (inv_chan * (norm_grad - first_chan - normed * second_chan)).astype(jnp.bfloat16)
    flat_grads = cotangent.reshape(num_cells, -1)
    term_list = []
    for tap_t, tap_h, tap_w in tap_list:
        window_h = upsampled[
            tap_t : tap_t + frames, tap_h : tap_h + up_rows, tap_w : tap_w + up_cols
        ].reshape(num_cells, channels)
        term_list.append(
            lax.dot_general(
                window_h, flat_grads, (((0,), (0,)), ((), ())), preferred_element_type=jnp.float32
            )
        )
    whole_terms = jnp.stack(term_list, 1)
    whole_terms = lax.psum(whole_terms, "block")
    d_weights = lax.psum_scatter(whole_terms, "tile", scatter_dimension=0, tiled=True)
    return (d_acts, d_weights)


def solution(mesh):
    placed = (
        P("block", "tile", None, None),
        P(),
        P(),
        P("tile", None, None),
        P("block", "tile", None, None),
    )
    return jax.shard_map(
        shards,
        mesh=mesh,
        in_specs=placed,
        out_specs=(P("block", "tile", None, None), P("tile", None, None)),
        check_vma=False,
    )
```

profile of v0, /device:TPU:2, one launch (start us, length us, event | category | flops | bytes accessed | tf_op | source)
XLA Modules:
  0.0 430.7 jit_solution(1480891718286037013)
XLA Ops:
  11.7 56.1 %all-reduce.3 = (f32[2,32]{1,0:T(2,128)S(1)}, f32[2,32]{1,0:T(2,128)S(1)}) all-reduce(f32[2,32]{1,0:T(2,128)S(1)} %reduce_sum.86, f32[2,32]{1,0:T(2,128)S(1)} %reduce_sum.84), channel_id=1, replica_groups=mesh['block'=8,'tile'=32] {'tile'}, use_global_device_ids=true, to_apply=%region_5.0 | all-reduce | flops 128 | bytes 1024 | tf_op jit(solution)/shard_map/psum | solution.py:41
  68.8 1.9 collective-permute-start.1
  70.8 5.8 %collective-permute-start.2 = (bf16[4,1,128,192]{2,3,1,0:T(8,128)(2,1)S(1)}, bf16[4,1,128,192]{2,3,1,0:T(8,128)(2,1)S(1)}, u32[]{:S(2)}, u32[]{:S(2)}) collective-permute-start(bf16[4,1,128,192]{2,3,1,0:T(8,128)(2,1)S(1)} %get-tuple-element.44), channel_id=1, source_target_pairs={{1,0},{2,1},{3,2},{4,3},{5,4},{6,5},{7,6},{8,7},{9,8},{10,9},{11,1... | collective-permute-start | bytes 589832 | tf_op jit(solution)/shard_map/ppermute | solution.py:24
  77.9 1.8 collective-permute-done.2
  83.8 2.5 fusion.110
  88.0 1.8 copy.86
  90.8 1.8 copy.85
  92.6 1.7 copy.112
  94.3 1.8 copy.83
  96.1 1.7 copy.110
  97.7 1.8 copy.82
  99.5 1.7 copy.109
  101.2 1.8 copy.80
  103.0 1.7 copy.107
  104.7 1.8 copy.79
  106.5 1.7 copy.106
  108.2 1.8 copy.77
  110.0 1.7 copy.104
  111.7 1.8 copy.76
  113.5 1.7 copy.103
  115.2 1.8 copy.74
  117.0 1.7 copy.101
  118.7 1.8 copy.73
  120.5 1.7 copy.100
  122.1 1.8 copy.71
  123.9 1.7 copy.98
  125.6 1.8 copy.70
  127.4 1.7 copy.97
  129.1 1.8 copy.68
  132.5 1.8 copy.67
  134.3 1.7 copy.94
  136.0 1.8 copy.65
  137.8 1.7 copy.92
  139.5 9.7 %concatenate.111 = bf16[2,1,2,64,2,5184]{5,3,4,2,0,1:T(8,128)(2,1)} concatenate(bf16[2,1,2,64,2,192]{5,3,4,2,0,1:T(8,128)(2,1)} %copy.92, bf16[2,1,2,64,2,192]{5,3,4,2,0,1:T(8,128)(2,1)S(1)} %copy.93, bf16[2,1,2,64,2,192]{5,3,4,2,0,1:T(8,128)(2,1)} %copy.94, bf16[2,1,2,64,2,192]{5,3,4,2,0,1:T(8,128)(2,1)} %copy.95, bf16[2,1,2,64,2,192]{5,3,4,2,0,1:T(8,128)(2,1)S(1)} %copy.96, ...), dimensions={5} | concatenate | bytes 10616832 | tf_op jit(solution)/shard_map/concatenate | solution.py:71
  149.2 8.6 %copy.119 = bf16[384,27,192]{0,2,1:T(8,128)(2,1)} copy(bf16[384,27,192]{2,1,0:T(8,128)(2,1)} %all-gather.2.cloned.1.call-done) | data formatting | bytes 7962624 | tf_op jit(solution)/shard_map/all_gather | solution.py:72
  157.8 6.7 %fusion.8 = f32[2,64,384]{2,1,0:T(8,128)S(1)} fusion(bf16[384,5184,1,1,1]{0,1,4,3,2:T(8,128)(2,1)} %bitcast.286, bf16[2,1,2,64,2,5184]{5,3,4,2,0,1:T(8,128)(2,1)} %concatenate.111), kind=kOutput, calls=%fused_computation.10 | convolution fusion | flops 2038579200 | bytes 9486336 | tf_op jit(solution)/shard_map/dot_general | solution.py:74
  164.7 4.4 %collective-permute-start.3 = (bf16[2,1,64,384]{3,2,1,0:T(8,128)(2,1)S(1)}, bf16[2,1,64,384]{3,2,1,0:T(8,128)(2,1)S(1)}, u32[]{:S(2)}, u32[]{:S(2)}) collective-permute-start(bf16[2,1,64,384]{3,2,1,0:T(8,128)(2,1)S(1)} %get-tuple-element.45), channel_id=1, source_target_pairs={{0,32},{32,64},{64,96},{96,128},{128,160},{160,192},{192,224},{1,3... | collective-permute-start | bytes 294920 | tf_op jit(solution)/shard_map/ppermute | solution.py:13
  169.1 2.2 collective-permute-done.3
  171.3 5.1 %collective-permute-start.5 = (bf16[4,1,64,384]{3,2,1,0:T(8,128)(2,1)S(1)}, bf16[4,1,64,384]{3,2,1,0:T(8,128)(2,1)S(1)}, u32[]{:S(2)}, u32[]{:S(2)}) collective-permute-start(bf16[4,1,64,384]{3,2,1,0:T(8,128)(2,1)S(1)} %pad_maximum_fusion.3), channel_id=1, source_target_pairs={{1,0},{2,1},{3,2},{4,3},{5,4},{6,5},{7,6},{8,7},{9,8},{10,9},{11,1... | collective-permute-start | bytes 589832 | tf_op jit(solution)/shard_map/ppermute | solution.py:24
  176.4 2.1 collective-permute-start.4
  179.5 5.9 %collective-permute-done.4 = bf16[4,1,64,384]{3,2,1,0:T(8,128)(2,1)S(1)} collective-permute-done((bf16[4,1,64,384]{3,2,1,0:T(8,128)(2,1)S(1)}, bf16[4,1,64,384]{3,2,1,0:T(8,128)(2,1)S(1)}, u32[]{:S(2)}, u32[]{:S(2)}) %collective-permute-start.4) | collective-permute-done | bytes 196640 | tf_op jit(solution)/shard_map/ppermute | solution.py:23
  185.7 3.2 broadcast_in_dim.26
  188.9 5.1 %reshape.166 = bf16[4,6,128,384]{3,2,1,0:T(8,128)(2,1)S(1)} reshape(bf16[4,6,64,2,384]{4,3,2,1,0:T(2,128)(2,1)} %broadcast_in_dim.26) | data formatting | bytes 4718592 | tf_op jit(solution)/shard_map/reshape | solution.py:53
  220.9 12.0 %copy.120 = f32[384,27,192]{2,1,0:T(8,128)} copy(f32[384,27,192]{0,2,1:T(8,128)} %fusion.11) | data formatting | bytes 15925248 | tf_op jit(solution)/shard_map/stack | solution.py:98
  233.4 53.0 %all-reduce.2 = (f32[2,32]{1,0:T(2,128)S(1)}, f32[2,32]{1,0:T(2,128)S(1)}) all-reduce(f32[2,32]{1,0:T(2,128)S(1)} %reduce_sum.92, f32[2,32]{1,0:T(2,128)S(1)} %reduce_sum.90), channel_id=1, replica_groups=mesh['block'=8,'tile'=32] {'tile'}, use_global_device_ids=true, to_apply=%region_12.13 | all-reduce | flops 128 | bytes 1024 | tf_op jit(solution)/shard_map/psum | solution.py:83
  286.4 60.6 %reduce-scatter.2.cloned.1.call-done = f32[12,27,192]{2,1,0:T(8,128)} async-done(((f32[384,27,192]{2,1,0:T(8,128)}), f32[12,27,192]{2,1,0:T(8,128)}) %reduce-scatter.2.cloned.1.call-update) | async-done | bytes 248848 | tf_op jit(solution)/shard_map/reduce_scatter | solution.py:100
  348.1 74.3 %all-reduce.6.cloned.1.call-done = f32[12,27,192]{2,1,0:T(8,128)} async-done(((f32[12,27,192]{2,1,0:T(8,128)}), f32[12,27,192]{2,1,0:T(8,128)}) %all-reduce.6.cloned.1.call-update) | async-done | bytes 248848 | tf_op jit(solution)/shard_map/psum | solution.py:99
  422.4 1.8 copy.177
  (102 shorter events, 45.1 us)
Async XLA Ops:
  7.2 142.0 %all-gather.2.cloned.1.call-start = ((), (), s32[]{:S(2)}) async-start(), calls=%async_computation.1 | async-start | bytes 6488064 | tf_op jit(solution)/shard_map/all_gather | solution.py:72
  7.9 339.1 %reduce-scatter.2.cloned.1.call-start = ((), (), s32[]{:S(2)}) async-start(), calls=%async_computation.2 | async-start | bytes 12976128 | tf_op jit(solution)/shard_map/reduce_scatter | solution.py:100
  7.9 60.8 %collective-permute-start = (bf16[2,2,128,192]{2,3,1,0:T(8,128)(2,1)}, bf16[2,2,128,192]{2,3,1,0:T(8,128)(2,1)S(1)}, u32[]{:S(2)}, u32[]{:S(2)}) collective-permute-start(bf16[2,2,128,192]{2,3,1,0:T(8,128)(2,1)} %param.9), channel_id=1, source_target_pairs={{32,0},{64,32},{96,64},{128,96},{160,128},{192,160},{224,192},{33,... | collective-permute-start | bytes 589832 | tf_op jit(solution)/shard_map/ppermute | solution.py:13
  68.8 9.1 %collective-permute-start.1 = (bf16[4,1,128,192]{2,3,1,0:T(8,128)(2,1)S(1)}, bf16[4,1,128,192]{2,3,1,0:T(8,128)(2,1)S(1)}, u32[]{:S(2)}, u32[]{:S(2)}) collective-permute-start(bf16[4,1,128,192]{2,3,1,0:T(8,128)(2,1)S(1)} %get-tuple-element.43), channel_id=1, source_target_pairs={{0,1},{1,2},{2,3},{3,4},{4,5},{5,6},{6,7},{7,8},{8,9},{9,10},{10,1... | collective-permute-start | bytes 589832 | tf_op jit(solution)/shard_map/ppermute | solution.py:23
  70.8 8.9 %collective-permute-start.2 = (bf16[4,1,128,192]{2,3,1,0:T(8,128)(2,1)S(1)}, bf16[4,1,128,192]{2,3,1,0:T(8,128)(2,1)S(1)}, u32[]{:S(2)}, u32[]{:S(2)}) collective-permute-start(bf16[4,1,128,192]{2,3,1,0:T(8,128)(2,1)S(1)} %get-tuple-element.44), channel_id=1, source_target_pairs={{1,0},{2,1},{3,2},{4,3},{5,4},{6,5},{7,6},{8,7},{9,8},{10,9},{11,1... | collective-permute-start | bytes 589832 | tf_op jit(solution)/shard_map/ppermute | solution.py:24
  157.7 6.7 %copy-start.1 = (bf16[2,1,64,384]{3,2,1,0:T(8,128)(2,1)S(1)}, bf16[2,1,64,384]{3,2,1,0:T(8,128)(2,1)}, u32[]{:S(2)}) copy-start(bf16[2,1,64,384]{3,2,1,0:T(8,128)(2,1)} %param.5) | copy-start | bytes 294916
  157.7 6.7 %copy-start.2 = (f32[384]{0:T(512)S(1)}, f32[384]{0:T(512)}, u32[]{:S(2)}) copy-start(f32[384]{0:T(512)} %param.7) | copy-start | bytes 4612
  157.8 6.7 %copy-start.3 = (f32[384]{0:T(512)S(1)}, f32[384]{0:T(512)}, u32[]{:S(2)}) copy-start(f32[384]{0:T(512)} %param.6) | copy-start | bytes 4612
  164.7 6.6 %collective-permute-start.3 = (bf16[2,1,64,384]{3,2,1,0:T(8,128)(2,1)S(1)}, bf16[2,1,64,384]{3,2,1,0:T(8,128)(2,1)S(1)}, u32[]{:S(2)}, u32[]{:S(2)}) collective-permute-start(bf16[2,1,64,384]{3,2,1,0:T(8,128)(2,1)S(1)} %get-tuple-element.45), channel_id=1, source_target_pairs={{0,32},{32,64},{64,96},{96,128},{128,160},{160,192},{192,224},{1,3... | collective-permute-start | bytes 294920 | tf_op jit(solution)/shard_map/ppermute | solution.py:13
  171.3 8.2 %collective-permute-start.5 = (bf16[4,1,64,384]{3,2,1,0:T(8,128)(2,1)S(1)}, bf16[4,1,64,384]{3,2,1,0:T(8,128)(2,1)S(1)}, u32[]{:S(2)}, u32[]{:S(2)}) collective-permute-start(bf16[4,1,64,384]{3,2,1,0:T(8,128)(2,1)S(1)} %pad_maximum_fusion.3), channel_id=1, source_target_pairs={{1,0},{2,1},{3,2},{4,3},{5,4},{6,5},{7,6},{8,7},{9,8},{10,9},{11,1... | collective-permute-start | bytes 589832 | tf_op jit(solution)/shard_map/ppermute | solution.py:24
  176.4 9.1 %collective-permute-start.4 = (bf16[4,1,64,384]{3,2,1,0:T(8,128)(2,1)S(1)}, bf16[4,1,64,384]{3,2,1,0:T(8,128)(2,1)S(1)}, u32[]{:S(2)}, u32[]{:S(2)}) collective-permute-start(bf16[4,1,64,384]{3,2,1,0:T(8,128)(2,1)S(1)} %pad_maximum_fusion.3), channel_id=1, source_target_pairs={{0,1},{1,2},{2,3},{3,4},{4,5},{5,6},{6,7},{7,8},{8,9},{9,10},{10,1... | collective-permute-start | bytes 589832 | tf_op jit(solution)/shard_map/ppermute | solution.py:23
  188.9 5.3 %copy-start = (bf16[2,2,128,192]{2,3,1,0:T(8,128)(2,1)S(1)}, bf16[2,2,128,192]{2,3,1,0:T(8,128)(2,1)}, u32[]{:S(2)}) copy-start(bf16[2,2,128,192]{2,3,1,0:T(8,128)(2,1)} %param.9) | copy-start | bytes 589828
  232.9 189.4 %all-reduce.6.cloned.1.call-start = ((), (), s32[]{:S(2)}) async-start(), calls=%async_computation.3 | async-start | bytes 786432 | tf_op jit(solution)/shard_map/psum | solution.py:99
Sparse Core Ops, SparseCore 0:
  10.5 56.0 all-gather.1
  233.1 113.8 reduce-scatter.1
  349.3 72.9 all-reduce.5
where the time goes:
time: 433 us; the launch traced here: 431 us
  waiting for transfers between devices  147 us (34%)
  blocking collectives  109 us (25%)
  local copies, waits for them, and re-layouts  102 us (24%)
  matrix products  33.4 us (8%)
  starting transfers between devices  20.7 us (5%)
  between operations  14.2 us (3%)
    psum x1, waiting for transfers between devices, shards(): whole_terms = lax.psum(whole_terms, 'block')  74.3 us
    reduce_scatter x1, waiting for transfers between devices, shards(): lax.psum_scatter(whole_terms, 'tile', scatter_dimension=0, tiled=True)  60.6 us
    psum x1, blocking collectives, shards(): stat_sum, stat_sq = lax.psum((stat_sum, stat_sq), 'tile')  56.1 us
    psum x1, blocking collectives, shards(): first_sum, second_sum = lax.psum((first_sum, second_sum), 'tile')  53 us
    concatenate x28, local copies, waits for them, and re-layouts, shards(): columns = jnp.concatenate(windows, 1)  34.5 us
    slice x26, local copies, waits for them, and re-layouts, shards(): grad_field[2 - tap_t:2 - tap_t + frames, 2 - tap_h:2 - tap_h + up_rows, 2...  33.3 us
    dot_general x27, matrix products, shards(): lax.dot_general(window_h, flat_grads, (((0,), (0,)), ((), ())), preferred...  26.7 us
    another operation x1, local copies, waits for them, and re-layouts, shards(): whole_terms = jnp.stack(term_list, 1)  12 us
  transfers between devices with their start and end apart: 9, of which 7 were waited for; matrix products, arithmetic and copies ran while one was open for 17% of the time, Pallas kernels for 0%

commit v1 on v0

--- a/solution.py
+++ b/solution.py
@@ -5,6 +5,15 @@
 
 GROUPS = 32
 norm_eps = 1e-06
+
+
+def sum_by_hops(x, name):
+    size = lax.axis_size(name)
+    total, far = (x, 1)
+    while far < size:
+        total = total + lax.ppermute(total, name, [(i, i ^ far) for i in range(size)])
+        far = 2 * far
+    return total
 
 
 def from_behind(value, axis, steps):
@@ -96,7 +105,7 @@
             )
         )
     whole_terms = jnp.stack(term_list, 1)
-    whole_terms = lax.psum(whole_terms, "block")
+    whole_terms = sum_by_hops(whole_terms, "block")
     d_weights = lax.psum_scatter(whole_terms, "tile", scatter_dimension=0, tiled=True)
     return (d_acts, d_weights)
 

time: 433 us -> 1220 us (2.82)
  waiting for transfers between devices: 147 us -> 912 us
  other arithmetic: 3.85 us -> 25 us
  matrix products: 33.4 us -> 14 us
  starting transfers between devices: 20.7 us -> 33.4 us
    ppermute x0 -> x3, waiting for transfers between devices: none -> 845 us  [sum_by_hops(): lax.ppermute(total, name, [(i, i ^ far) for i in range(size)])]
    psum x1 -> x0, waiting for transfers between devices: 74.3 us -> none  [shards(): whole_terms = lax.psum(whole_terms, 'block')]
    add x0 -> x3, other arithmetic: none -> 21.2 us  [sum_by_hops(): total + lax.ppermute(total, name, [(i, i ^ far) for i in range(size)])]
    dot_general x27, matrix products: 26.7 us -> 7.25 us  [shards(): lax.dot_general(window_h, flat_grads, (((0,), (0,)), ((), ())), preferred...]
    ppermute x0 -> x3, starting transfers between devices: none -> 12.8 us  [sum_by_hops(): lax.ppermute(total, name, [(i, i ^ far) for i in range(size)])]
  transfers between devices with their start and end apart: 9 -> 11, of which waited for: 7 -> 9; matrix products, arithmetic and copies ran while one was open for 17% -> 6% of each run, Pallas kernels for 0% -> 0%
where the time goes in v1:
time: 1220 us
  waiting for transfers between devices  912 us (75%)
  blocking collectives  117 us (10%)
  local copies, waits for them, and re-layouts  101 us (8%)
  starting transfers between devices  33.4 us (3%)
  other arithmetic  25 us (2%)
  between operations  14.6 us (1%)
  matrix products  14 us (1%)
    ppermute x3, waiting for transfers between devices, sum_by_hops(): lax.ppermute(total, name, [(i, i ^ far) for i in range(size)])  845 us
    psum x1, blocking collectives, shards(): first_sum, second_sum = lax.psum((first_sum, second_sum), 'tile')  60.8 us
    psum x1, blocking collectives, shards(): stat_sum, stat_sq = lax.psum((stat_sum, stat_sq), 'tile')  56.1 us
    reduce_scatter x1, waiting for transfers between devices, shards(): lax.psum_scatter(whole_terms, 'tile', scatter_dimension=0, tiled=True)  55.1 us
    concatenate x28, local copies, waits for them, and re-layouts, shards(): columns = jnp.concatenate(windows, 1)  34.5 us
    slice x26, local copies, waits for them, and re-layouts, shards(): grad_field[2 - tap_t:2 - tap_t + frames, 2 - tap_h:2 - tap_h + up_rows, 2...  33.3 us
  transfers between devices with their start and end apart: 11, of which 9 were waited for; matrix products, arithmetic and copies ran while one was open for 6% of the time, Pallas kernels for 0%

profile of v1, /device:TPU:2, one launch (start us, length us, event | category | flops | bytes accessed | tf_op | source)
XLA Modules:
  0.0 1217.3 jit_solution(319310215338063853)
XLA Ops:
  11.7 56.1 %all-reduce.3 = (f32[2,32]{1,0:T(2,128)S(1)}, f32[2,32]{1,0:T(2,128)S(1)}) all-reduce(f32[2,32]{1,0:T(2,128)S(1)} %reduce_sum.86, f32[2,32]{1,0:T(2,128)S(1)} %reduce_sum.84), channel_id=1, replica_groups=mesh['block'=8,'tile'=32] {'tile'}, use_global_device_ids=true, to_apply=%region_5.0 | all-reduce | flops 128 | bytes 1024 | tf_op jit(solution)/shard_map/psum | solution.py:50
  68.8 1.9 collective-permute-start.1
  70.8 5.8 collective-permute-start.2
  77.9 1.8 collective-permute-done.2
  83.8 2.5 fusion.110
  88.0 1.8 copy.86
  90.8 1.8 copy.85
  94.3 1.8 copy.83
  97.7 1.8 copy.82
  101.2 1.8 copy.80
  103.0 1.7 copy.107
  104.7 1.8 copy.79
  106.5 1.7 copy.106
  108.2 1.8 copy.77
  110.0 1.7 copy.104
  111.7 1.8 copy.76
  113.5 1.7 copy.103
  115.2 1.8 copy.74
  117.0 1.7 copy.101
  118.7 1.8 copy.73
  122.1 1.8 copy.71
  125.6 1.8 copy.70
  129.1 1.8 copy.68
  132.5 1.8 copy.67
  134.3 1.7 copy.94
  136.0 1.8 copy.65
  139.5 9.7 concatenate.111
  149.2 8.6 copy.119
  157.8 6.7 fusion.8
  164.7 4.4 collective-permute-start.3
  169.1 2.2 collective-permute-done.3
  171.3 5.1 collective-permute-start.5
  176.4 2.1 collective-permute-start.4
  179.5 5.9 collective-permute-done.4
  185.7 3.2 broadcast_in_dim.26
  188.9 5.1 reshape.166
  201.6 2.2 collective-permute-start.6
  204.7 165.0 %collective-permute-done.6 = f32[384,27,192]{0,2,1:T(8,128)} collective-permute-done((f32[384,27,192]{0,2,1:T(8,128)S(1)}, f32[384,27,192]{0,2,1:T(8,128)}, u32[]{:S(2)}, u32[]{:S(2)}) %collective-permute-start.6) | collective-permute-done | bytes 7962656 | tf_op jit(solution)/shard_map/ppermute | solution.py:14
  369.6 6.4 add.49
  376.0 4.4 collective-permute-start.7
  380.4 335.9 %collective-permute-done.7 = f32[384,27,192]{0,2,1:T(8,128)} collective-permute-done((f32[384,27,192]{0,2,1:T(8,128)S(1)}, f32[384,27,192]{0,2,1:T(8,128)}, u32[]{:S(2)}, u32[]{:S(2)}) %collective-permute-start.7) | collective-permute-done | bytes 7962656 | tf_op jit(solution)/shard_map/ppermute | solution.py:14
  716.3 7.4 add.50
  723.7 6.2 collective-permute-start.8
  730.0 343.7 %collective-permute-done.8 = f32[384,27,192]{0,2,1:T(8,128)S(1)} collective-permute-done((f32[384,27,192]{0,2,1:T(8,128)}, f32[384,27,192]{0,2,1:T(8,128)S(1)}, u32[]{:S(2)}, u32[]{:S(2)}) %collective-permute-start.8) | collective-permute-done | bytes 7962656 | tf_op jit(solution)/shard_map/ppermute | solution.py:14
  1073.7 7.4 add.51
  1081.1 12.0 copy.120
  1093.5 60.8 %all-reduce.2 = (f32[2,32]{1,0:T(2,128)S(1)}, f32[2,32]{1,0:T(2,128)S(1)}) all-reduce(f32[2,32]{1,0:T(2,128)S(1)} %reduce_sum.92, f32[2,32]{1,0:T(2,128)S(1)} %reduce_sum.90), channel_id=1, replica_groups=mesh['block'=8,'tile'=32] {'tile'}, use_global_device_ids=true, to_apply=%region_12.13 | all-reduce | flops 128 | bytes 1024 | tf_op jit(solution)/shard_map/psum | solution.py:92
  1155.4 55.1 %reduce-scatter.2.cloned.1.call-done = f32[12,27,192]{2,1,0:T(8,128)} async-done(((f32[384,27,192]{2,1,0:T(8,128)}), f32[12,27,192]{2,1,0:T(8,128)}) %reduce-scatter.2.cloned.1.call-update) | async-done | bytes 248848 | tf_op jit(solution)/shard_map/reduce_scatter | solution.py:109
  (109 shorter events, 38.1 us)
Async XLA Ops:
  7.2 142.0 %all-gather.2.cloned.1.call-start = ((), (), s32[]{:S(2)}) async-start(), calls=%async_computation.1 | async-start | bytes 6488064 | tf_op jit(solution)/shard_map/all_gather | solution.py:81
  7.9 1202.6 %reduce-scatter.2.cloned.1.call-start = ((), (), s32[]{:S(2)}) async-start(), calls=%async_computation.2 | async-start | bytes 12976128 | tf_op jit(solution)/shard_map/reduce_scatter | solution.py:109
  7.9 60.8 %collective-permute-start = (bf16[2,2,128,192]{2,3,1,0:T(8,128)(2,1)}, bf16[2,2,128,192]{2,3,1,0:T(8,128)(2,1)S(1)}, u32[]{:S(2)}, u32[]{:S(2)}) collective-permute-start(bf16[2,2,128,192]{2,3,1,0:T(8,128)(2,1)} %param.9), channel_id=1, source_target_pairs={{32,0},{64,32},{96,64},{128,96},{160,128},{192,160},{224,192},{33,... | collective-permute-start | bytes 589832 | tf_op jit(solution)/shard_map/ppermute | solution.py:22
  68.8 9.1 collective-permute-start.1
  70.8 8.9 collective-permute-start.2
  157.7 6.7 copy-start.2
  157.7 6.7 copy-start.3
  157.8 6.7 copy-start.4
  164.7 6.6 collective-permute-start.3
  171.3 8.2 collective-permute-start.5
  176.4 9.1 collective-permute-start.4
  188.9 5.3 copy-start
  201.6 3.1 copy-start.1
  201.6 168.1 %collective-permute-start.6 = (f32[384,27,192]{0,2,1:T(8,128)S(1)}, f32[384,27,192]{0,2,1:T(8,128)}, u32[]{:S(2)}, u32[]{:S(2)}) collective-permute-start(f32[384,27,192]{0,2,1:T(8,128)S(1)} %fusion.11), channel_id=1, source_target_pairs={{0,32},{32,0},{64,96},{96,64},{128,160},{160,128},{192,224},{224,1... | collective-permute-start | bytes 23887880 | tf_op jit(solution)/shard_map/ppermute | solution.py:14
  376.0 340.3 %collective-permute-start.7 = (f32[384,27,192]{0,2,1:T(8,128)S(1)}, f32[384,27,192]{0,2,1:T(8,128)}, u32[]{:S(2)}, u32[]{:S(2)}) collective-permute-start(f32[384,27,192]{0,2,1:T(8,128)S(1)} %add.49), channel_id=1, source_target_pairs={{0,64},{32,96},{64,0},{96,32},{128,192},{160,224},{192,128},{224,1... | collective-permute-start | bytes 23887880 | tf_op jit(solution)/shard_map/ppermute | solution.py:14
  723.7 350.0 %collective-permute-start.8 = (f32[384,27,192]{0,2,1:T(8,128)}, f32[384,27,192]{0,2,1:T(8,128)S(1)}, u32[]{:S(2)}, u32[]{:S(2)}) collective-permute-start(f32[384,27,192]{0,2,1:T(8,128)} %add.50), channel_id=1, source_target_pairs={{0,128},{32,160},{64,192},{96,224},{128,0},{160,32},{192,64},{224,... | collective-permute-start | bytes 23887880 | tf_op jit(solution)/shard_map/ppermute | solution.py:14
Sparse Core Ops, SparseCore 0:
  10.5 56.0 all-gather.1
  1093.2 117.2 reduce-scatter.1
